TPU v7x, 512 devices: a whole 4x8x8 slice. The times are simulated.
512 devices in a mesh: seq: 32 (over x, y), chan: 16 (over z, core).
Axes of the slice: x: 4, y: 8, z: 8, core: 2. Of those that a mesh axis runs over, the one named last changes fastest.
Arguments:
- tokens: bfloat16 [1536, 16384], P('chan', 'seq'), may hold values from -6 to 6
- gate_weight: bfloat16 [1536, 1536], P('chan'), may hold values from -0.15625 to 0.15625
- value_weight: bfloat16 [1536, 1536], P('chan'), may hold values from -0.15625 to 0.15625
- first_factor: bfloat16 [64, 256, 256], P('seq'), may hold values from -0.375 to 0.375
- second_factor: bfloat16 [256, 64, 64], P('seq'), may hold values from -0.75 to 0.75
- down_latent: bfloat16 [1536, 128], P('chan'), may hold values from -0.15625 to 0.15625
- up_latent: bfloat16 [1536, 128], P('chan'), may hold values from -0.5 to 0.5
- doc_lengths: int32 [64], replicated, may hold values from 1 to 8704, 16384 in all
- cotangent: bfloat16 [1536, 16384], P('chan', 'seq'), may hold values from -6 to 6
Outputs:
- hidden: bfloat16 [1536, 16384], P('chan', 'seq')
- d_gate_weight: float32 [1536, 1536], P('chan')
- d_value_weight: float32 [1536, 1536], P('chan')
- d_first: float32 [64, 256, 256], P('seq', 'chan')
- d_second: float32 [256, 64, 64], P('seq', 'chan')
- d_down: float32 [1536, 128], P('chan')
- d_up: float32 [1536, 128], P('chan')
Inputs may be any that keep to these rules, and one draw needn't show every extreme that they name: `doc_lengths`: the documents' lengths sum to 16384; the longest is exactly 8704 tokens.
All inputs are finite; a program needn't handle non-finite values.
Results may differ from a plain program's by a relative error of at most 0.0058.
Values may be sent and summed in bfloat16 or wider, within the bound.
No kernel may reach another device: no remote copies, remote signals or barrier semaphores. Data moves between devices by JAX's collectives and lax.ppermute only.
A program may use at most 64 MiB of HBM per device.

v0:
```python
import jax
import jax.numpy as jnp
from jax import lax
from jax.sharding import PartitionSpec as P

HIGHEST = lax.Precision.HIGHEST


def seq_exchange(x):
    return lax.all_to_all(x, "seq", 0, 0, tiled=True)


def chan_exchange(x):
    return lax.all_to_all(x, "chan", 0, 0, tiled=True)


def body(
    tokens,
    gate_weight,
    value_weight,
    first_factor,
    second_factor,
    down_latent,
    up_latent,
    doc_lengths,
    cotangent,
):
    n_seq = lax.axis_size("seq")
    n_chan = lax.axis_size("chan")
    chan_rows, tok_cols = tokens.shape
    blocks_here, block_width, _ = first_factor.shape
    k_here, n_blk2, _ = second_factor.shape
    lat = down_latent.shape[1]
    n_doc = doc_lengths.shape[0]
    docs_here = n_doc // n_seq
    me = lax.axis_index("seq")
    packed = jnp.concatenate([tokens, down_latent], axis=1)
    gathered_all = lax.all_gather(packed, "chan", axis=0, tiled=True)
    gathered = gathered_all[:, :tok_cols]
    down_full = gathered_all[:, tok_cols:]
    doc_ends = jnp.cumsum(doc_lengths)
    doc_begins = doc_ends - doc_lengths
    position = me * tok_cols + jnp.arange(tok_cols, dtype=jnp.int32)
    member = (
        (position[None, :] >= doc_begins[:, None]) & (position[None, :] < doc_ends[:, None])
    ).astype(jnp.float32)
    len_scale = lax.rsqrt(doc_lengths.astype(jnp.float32))
    gate_pre = jnp.dot(gate_weight, gathered, preferred_element_type=jnp.float32)
    value_bf = jnp.dot(value_weight, gathered, preferred_element_type=jnp.float32).astype(
        jnp.bfloat16
    )
    latent = jnp.einsum("ct,cl->lt", gathered, down_full, preferred_element_type=jnp.float32)
    doc_lat_part = jnp.einsum("dt,lt->dl", member, latent, precision=HIGHEST)
    xdoc_part = jnp.einsum(
        "ct,dt->cd", tokens, member.astype(jnp.bfloat16), preferred_element_type=jnp.float32
    )
    blocked = value_bf.reshape(chan_rows, blocks_here, block_width)
    inner_mix = jnp.einsum(
        "ikj,cij->ikc", first_factor, blocked, preferred_element_type=jnp.float32
    ).astype(jnp.bfloat16)
    sig = jax.nn.sigmoid(gate_pre)
    act = gate_pre * sig
    upstream = cotangent.astype(jnp.float32)
    d_mixed = upstream * act
    d_mixed_bf = d_mixed.astype(jnp.bfloat16)
    per_doc_part = jnp.einsum("ct,dt->cd", d_mixed, member, precision=HIGHEST)
    inner_send = inner_mix.reshape(blocks_here, n_seq, k_here, chan_rows).transpose(1, 0, 2, 3)
    d_send = d_mixed_bf.reshape(chan_rows, blocks_here, n_seq, k_here).transpose(2, 1, 3, 0)
    recv2 = seq_exchange(jnp.concatenate([inner_send, d_send], axis=3))
    columns = recv2[..., :chan_rows].reshape(n_seq * blocks_here, k_here, chan_rows)
    d_outer = recv2[..., chan_rows:].reshape(n_seq * blocks_here, k_here, chan_rows)
    small_send = jnp.concatenate(
        [
            doc_lat_part.reshape(n_seq, docs_here * lat),
            per_doc_part.reshape(chan_rows, n_seq, docs_here)
            .transpose(1, 0, 2)
            .reshape(n_seq, chan_rows * docs_here),
            xdoc_part.reshape(chan_rows, n_seq, docs_here)
            .transpose(1, 0, 2)
            .reshape(n_seq, chan_rows * docs_here),
        ],
        axis=1,
    )
    small_red = jnp.sum(seq_exchange(small_send), axis=0)
    n_a = docs_here * lat
    n_b = chan_rows * docs_here
    scale_here = lax.dynamic_slice(len_scale, (me * docs_here,), (docs_here,))
    pooled_here = small_red[:n_a].reshape(docs_here, lat) * scale_here[:, None]
    per_doc_here = small_red[n_a : n_a + n_b].reshape(chan_rows, docs_here)
    xdoc_here = small_red[n_a + n_b :].reshape(chan_rows, docs_here)
    up_float = up_latent.astype(jnp.float32)
    g_part = jnp.einsum("cd,cl->dl", per_doc_here, up_float, precision=HIGHEST)
    g_here = jnp.sum(chan_exchange(jnp.broadcast_to(g_part.reshape(1, n_a), (n_chan, n_a))), axis=0)
    outer_mix = jnp.einsum(
        "kmi,ikc->mkc", second_factor, columns, preferred_element_type=jnp.float32
    ).astype(jnp.bfloat16)
    d_inner = jnp.einsum(
        "kmi,mkc->ikc", second_factor, d_outer, preferred_element_type=jnp.float32
    ).astype(jnp.bfloat16)
    d_second_part = jnp.einsum("mkc,ikc->kmi", d_outer, columns, preferred_element_type=jnp.float32)
    outer_send = outer_mix.reshape(n_seq, blocks_here, k_here, chan_rows)
    dinner_send = d_inner.reshape(n_seq, blocks_here, k_here, chan_rows)
    recv3 = seq_exchange(jnp.concatenate([outer_send, dinner_send], axis=3))
    outer_tok = (
        recv3[..., :chan_rows]
        .transpose(3, 1, 0, 2)
        .reshape(chan_rows, tok_cols)
        .astype(jnp.float32)
    )
    d_rows = (
        recv3[..., chan_rows:].transpose(1, 0, 2, 3).reshape(blocks_here, n_seq * k_here, chan_rows)
    )
    piece = jnp.concatenate(
        [pooled_here.reshape(n_a), per_doc_here.reshape(n_b), xdoc_here.reshape(n_b)]
    )
    gath3 = seq_exchange(jnp.broadcast_to(piece[None, :], (n_seq, piece.shape[0])))
    pooled = gath3[:, :n_a].reshape(n_doc, lat)
    per_doc = (
        gath3[:, n_a : n_a + n_b]
        .reshape(n_seq, chan_rows, docs_here)
        .transpose(1, 0, 2)
        .reshape(chan_rows, n_doc)
    )
    xdoc = (
        gath3[:, n_a + n_b :]
        .reshape(n_seq, chan_rows, docs_here)
        .transpose(1, 0, 2)
        .reshape(chan_rows, n_doc)
    )
    spread = jnp.einsum("dl,cl->cd", pooled, up_float, precision=HIGHEST)
    summary = jnp.dot(spread, member, precision=HIGHEST)
    mixed = outer_tok + summary
    hidden = (act * mixed).astype(jnp.bfloat16)
    d_gate_bf = (upstream * mixed * sig * (1.0 + gate_pre * (1.0 - sig))).astype(jnp.bfloat16)
    d_value_bf = (
        jnp.einsum("ikj,ikc->cij", first_factor, d_rows, preferred_element_type=jnp.float32)
        .astype(jnp.bfloat16)
        .reshape(chan_rows, tok_cols)
    )
    d_first_part = jnp.einsum("ikc,cij->ikj", d_rows, blocked, preferred_element_type=jnp.float32)
    d_up = jnp.einsum("cd,dl->cl", per_doc, pooled, precision=HIGHEST)
    both_grads = jnp.concatenate([d_gate_bf, d_value_bf], axis=0)
    d_proj_part = jnp.einsum("ot,it->oi", both_grads, gathered, preferred_element_type=jnp.float32)
    rows_here = 2 * chan_rows // n_seq
    width = d_proj_part.shape[1]
    proj_red = jnp.sum(seq_exchange(d_proj_part.reshape(n_seq, rows_here, width)), axis=0)
    k_part = block_width // n_chan
    m_part = n_blk2 // n_chan
    first_send = (
        d_first_part.reshape(blocks_here, n_chan, k_part, block_width)
        .transpose(1, 0, 2, 3)
        .reshape(n_chan, -1)
    )
    second_send = (
        d_second_part.reshape(k_here, n_chan, m_part, n_blk2)
        .transpose(1, 0, 2, 3)
        .reshape(n_chan, -1)
    )
    fac_red = jnp.sum(chan_exchange(jnp.concatenate([first_send, second_send], axis=1)), axis=0)
    n_f = blocks_here * k_part * block_width
    d_first = fac_red[:n_f].reshape(blocks_here, k_part, block_width)
    d_second = fac_red[n_f:].reshape(k_here, m_part, n_blk2)
    piece5 = jnp.concatenate([proj_red.reshape(-1), g_here])
    gath5 = seq_exchange(jnp.broadcast_to(piece5[None, :], (n_seq, piece5.shape[0])))
    n_p = rows_here * width
    d_proj = gath5[:, :n_p].reshape(2 * chan_rows, width)
    d_pooled = gath5[:, n_p:].reshape(n_doc, lat) * len_scale[:, None]
    d_down = jnp.einsum(
        "cd,dl->cl", xdoc, d_pooled.astype(jnp.bfloat16).astype(jnp.float32), precision=HIGHEST
    )
    return (hidden, d_proj[:chan_rows], d_proj[chan_rows:], d_first, d_second, d_down, d_up)


def solution(mesh):
    in_specs = (
        P("chan", "seq"),
        P("chan", None),
        P("chan", None),
        P("seq", None, None),
        P("seq", None, None),
        P("chan", None),
        P("chan", None),
        P(),
        P("chan", "seq"),
    )
    out_specs = (
        P("chan", "seq"),
        P("chan", None),
        P("chan", None),
        P("seq", "chan", None),
        P("seq", "chan", None),
        P("chan", None),
        P("chan", None),
    )
    return jax.shard_map(body, mesh=mesh, in_specs=in_specs, out_specs=out_specs, check_vma=False)
```

profile of v0, /device:TPU:1, one launch (start us, length us, event | category | flops | bytes accessed | tf_op | source)
XLA Modules:
  0.0 258.2 jit_solution(9266337359368972084)
XLA Ops:
  7.2 1.6 pad_maximum_fusion.2
  8.9 0.7 copy.140
  9.8 0.7 sub.6
  10.5 1.1 fusion.27
  11.8 47.7 %all-gather.2.cloned.1.call-done = bf16[1536,640]{1,0:T(8,128)(2,1)} async-done(((bf16[96,640]{1,0:T(8,128)(2,1)}), bf16[1536,640]{1,0:T(8,128)(2,1)}) %all-gather.2.cloned.1.call-update) | async-done | bytes 1966096 | tf_op jit(solution)/shard_map/all_gather | solution.py:38
  59.4 2.1 fusion.4
  61.5 0.3 fusion.31
  61.8 0.4 fusion.17
  62.3 0.3 fusion.16
  62.7 0.2 copy-done.17
  63.1 0.7 all_to_all.39
  63.8 9.3 %all-to-all-start.2 = ((f32[32,1,640]{2,1,0:T(1,128)}), f32[32,1,640]{2,1,0:T(1,128)S(1)}, u32[]{:S(2)}, u32[]{:S(2)}) async-start(f32[32,1,640]{2,1,0:T(1,128)} %all_to_all.39), calls=%async_computation.2 | async-start | bytes 163840 | tf_op jit(solution)/shard_map/all_to_all | solution.py:10
  73.1 1.3 convolution_convert_fusion.2
  74.4 0.2 fusion
  74.7 0.1 copy.131
  74.8 0.3 copy-done.10
  75.2 0.1 pad_maximum_fusion
  75.3 0.7 copy.133
  76.0 6.0 %all-to-all-done.2 = f32[32,1,640]{2,1,0:T(1,128)S(1)} async-done(((f32[32,1,640]{2,1,0:T(1,128)}), f32[32,1,640]{2,1,0:T(1,128)S(1)}, u32[]{:S(2)}, u32[]{:S(2)}) %all-to-all-start.2) | async-done | bytes 81952 | tf_op jit(solution)/shard_map/all_to_all | solution.py:10
  82.0 3.9 %all-to-all-start = ((bf16[32,2,8,192]{3,2,1,0:T(8,128)(2,1)}), bf16[32,2,8,192]{3,2,1,0:T(8,128)(2,1)S(1)}, u32[]{:S(2)}, u32[]{:S(2)}) async-start(bf16[32,2,8,192]{3,2,1,0:T(8,128)(2,1)} %copy.133), calls=%async_computation | async-start | bytes 524288 | tf_op jit(solution)/shard_map/all_to_all | solution.py:10
  86.0 0.4 copy-done.14
  86.6 9.0 %all-to-all-done = bf16[32,2,8,192]{3,2,1,0:T(8,128)(2,1)S(1)} async-done(((bf16[32,2,8,192]{3,2,1,0:T(8,128)(2,1)}), bf16[32,2,8,192]{3,2,1,0:T(8,128)(2,1)S(1)}, u32[]{:S(2)}, u32[]{:S(2)}) %all-to-all-start) | async-done | bytes 196640 | tf_op jit(solution)/shard_map/all_to_all | solution.py:10
  95.5 0.7 broadcast_in_dim.8
  96.2 6.2 %all-to-all-start.3 = ((f32[32,1,640]{2,1,0:T(1,128)}), f32[32,1,640]{2,1,0:T(1,128)S(1)}, u32[]{:S(2)}, u32[]{:S(2)}) async-start(f32[32,1,640]{2,1,0:T(1,128)} %broadcast_in_dim.8), calls=%async_computation.3 | async-start | bytes 163840 | tf_op jit(solution)/shard_map/all_to_all | solution.py:10
  102.8 0.5 copy-done.2
  103.4 0.2 convolution_convert_fusion
  103.5 0.2 convolution_convert_fusion.1
  103.8 0.2 copy.137
  103.9 0.2 copy.138
  104.1 0.8 pad_maximum_fusion.1
  105.0 6.4 %all-to-all-done.3 = f32[32,1,640]{2,1,0:T(1,128)S(1)} async-done(((f32[32,1,640]{2,1,0:T(1,128)}), f32[32,1,640]{2,1,0:T(1,128)S(1)}, u32[]{:S(2)}, u32[]{:S(2)}) %all-to-all-start.3) | async-done | bytes 81952 | tf_op jit(solution)/shard_map/all_to_all | solution.py:10
  111.4 3.9 %all-to-all-start.1 = ((bf16[32,2,8,192]{3,2,1,0:T(8,128)(2,1)}), bf16[32,2,8,192]{3,2,1,0:T(8,128)(2,1)S(1)}, u32[]{:S(2)}, u32[]{:S(2)}) async-start(bf16[32,2,8,192]{3,2,1,0:T(8,128)(2,1)} %pad_maximum_fusion.1), calls=%async_computation.1 | async-start | bytes 524288 | tf_op jit(solution)/shard_map/all_to_all | solution.py:10
  115.3 0.1 reshape.211
  115.4 0.2 convolution_bitcast_fusion.1
  115.7 0.2 fusion.36
  115.8 9.2 %all-to-all-done.1 = bf16[32,2,8,192]{3,2,1,0:T(8,128)(2,1)S(1)} async-done(((bf16[32,2,8,192]{3,2,1,0:T(8,128)(2,1)}), bf16[32,2,8,192]{3,2,1,0:T(8,128)(2,1)S(1)}, u32[]{:S(2)}, u32[]{:S(2)}) %all-to-all-start.1) | async-done | bytes 196640 | tf_op jit(solution)/shard_map/all_to_all | solution.py:10
  125.0 0.6 broadcast_in_dim.10
  125.6 8.4 %all-to-all-start.5 = ((f32[16,1,256]{2,1,0:T(1,128)}), f32[16,1,256]{2,1,0:T(1,128)}, u32[]{:S(2)}, u32[]{:S(2)}) async-start(f32[16,1,256]{2,1,0:T(1,128)} %broadcast_in_dim.10), calls=%async_computation.5 | async-start | bytes 32768 | tf_op jit(solution)/shard_map/all_to_all | solution.py:14
  134.3 0.2 fusion.1
  134.5 1.9 fusion.11
  136.4 0.7 fusion.2
  137.1 1.3 reshape.209
  138.4 2.9 %all-to-all-done.5 = f32[16,1,256]{2,1,0:T(1,128)} async-done(((f32[16,1,256]{2,1,0:T(1,128)}), f32[16,1,256]{2,1,0:T(1,128)}, u32[]{:S(2)}, u32[]{:S(2)}) %all-to-all-start.5) | async-done | bytes 16416 | tf_op jit(solution)/shard_map/all_to_all | solution.py:14
  141.3 4.2 %all-to-all-start.4 = ((f32[32,6,1536]{2,1,0:T(8,128)}), f32[32,6,1536]{2,1,0:T(8,128)S(1)}, u32[]{:S(2)}, u32[]{:S(2)}) async-start(f32[32,6,1536]{2,1,0:T(8,128)} %reshape.209), calls=%async_computation.4 | async-start | bytes 3145728 | tf_op jit(solution)/shard_map/all_to_all | solution.py:10
  145.6 0.2 fusion.37
  145.8 0.2 reshape.215
  146.1 0.2 fusion.18
  146.4 0.3 copy.167
  146.7 1.5 copy.154
  148.2 33.8 %all-to-all-done.4 = f32[32,6,1536]{2,1,0:T(8,128)S(1)} async-done(((f32[32,6,1536]{2,1,0:T(8,128)}), f32[32,6,1536]{2,1,0:T(8,128)S(1)}, u32[]{:S(2)}, u32[]{:S(2)}) %all-to-all-start.4) | async-done | bytes 1179680 | tf_op jit(solution)/shard_map/all_to_all | solution.py:10
  182.1 7.8 %all-to-all-start.7 = ((f32[16,1,10240]{2,1,0:T(1,128)}), f32[16,1,10240]{2,1,0:T(1,128)S(1)}, u32[]{:S(2)}, u32[]{:S(2)}) async-start(f32[16,1,10240]{2,1,0:T(1,128)} %copy.154), calls=%async_computation.7 | async-start | bytes 1310720 | tf_op jit(solution)/shard_map/all_to_all | solution.py:14
  189.9 0.8 reduce_sum.38
  190.7 0.1 reduce_sum.37
  190.8 19.0 %all-to-all-done.7 = f32[16,1,10240]{2,1,0:T(1,128)S(1)} async-done(((f32[16,1,10240]{2,1,0:T(1,128)}), f32[16,1,10240]{2,1,0:T(1,128)S(1)}, u32[]{:S(2)}, u32[]{:S(2)}) %all-to-all-start.7) | async-done | bytes 655392 | tf_op jit(solution)/shard_map/all_to_all | solution.py:14
  209.9 1.7 broadcast_in_dim.11
  211.5 5.3 %all-to-all-start.6 = ((f32[32,1,9472]{2,1,0:T(1,128)}), f32[32,1,9472]{2,1,0:T(1,128)S(1)}, u32[]{:S(2)}, u32[]{:S(2)}) async-start(f32[32,1,9472]{2,1,0:T(1,128)} %broadcast_in_dim.11), calls=%async_computation.6 | async-start | bytes 2424832 | tf_op jit(solution)/shard_map/all_to_all | solution.py:10
  217.5 0.9 fusion.39
  218.4 0.4 reduce_sum.39
  218.8 0.6 reshape.216
  219.4 0.7 reshape.217
  220.1 28.2 %all-to-all-done.6 = f32[32,1,9472]{2,1,0:T(1,128)S(1)} async-done(((f32[32,1,9472]{2,1,0:T(1,128)}), f32[32,1,9472]{2,1,0:T(1,128)S(1)}, u32[]{:S(2)}, u32[]{:S(2)}) %all-to-all-start.6) | async-done | bytes 1212448 | tf_op jit(solution)/shard_map/all_to_all | solution.py:10
  248.6 0.9 slice.101
  249.5 0.9 slice.99
  250.5 0.9 fusion.38
  (79 shorter events, 2.7 us)
Async XLA Ops:
  7.2 54.6 %copy-start = (bf16[96,1536]{1,0:T(8,128)(2,1)S(1)}, bf16[96,1536]{1,0:T(8,128)(2,1)}, u32[]{:S(2)}) copy-start(bf16[96,1536]{1,0:T(8,128)(2,1)} %param.10) | copy-start | bytes 884740
  7.2 52.2 %all-gather.2.cloned.1.call-start = ((), (), s32[]{:S(2)}) async-start(), calls=%async_computation.8 | async-start | bytes 2088960 | tf_op jit(solution)/shard_map/all_gather | solution.py:38
  9.7 52.1 %copy-start.16 = (bf16[96,512]{1,0:T(8,128)(2,1)S(1)}, bf16[96,512]{1,0:T(8,128)(2,1)}, u32[]{:S(2)}) copy-start(bf16[96,512]{1,0:T(8,128)(2,1)} %param.17) | copy-start | bytes 294916
  59.4 2.4 copy-start.1
  62.3 0.7 copy-start.17
  62.6 11.8 %copy-start.8 = (bf16[2,256,256]{2,1,0:T(8,128)(2,1)S(1)}, bf16[2,256,256]{2,1,0:T(8,128)(2,1)}, u32[]{:S(2)}) copy-start(bf16[2,256,256]{2,1,0:T(8,128)(2,1)} %param.12) | copy-start | bytes 786436
  63.8 18.2 %all-to-all-start.2 = ((f32[32,1,640]{2,1,0:T(1,128)}), f32[32,1,640]{2,1,0:T(1,128)S(1)}, u32[]{:S(2)}, u32[]{:S(2)}) async-start(f32[32,1,640]{2,1,0:T(1,128)} %all_to_all.39), calls=%async_computation.2 | async-start | bytes 163840 | tf_op jit(solution)/shard_map/all_to_all | solution.py:10
  74.4 0.6 copy-start.10
  74.4 11.5 %copy-start.13 = (s32[64]{0:T(128)S(1)}, s32[64]{0:T(128)}, u32[]{:S(2)}) copy-start(s32[64]{0:T(128)} %param.16) | copy-start | bytes 772
  75.0 28.3 %copy-start.9 = (bf16[8,64,64]{2,1,0:T(8,128)(2,1)S(1)}, bf16[8,64,64]{2,1,0:T(8,128)(2,1)}, u32[]{:S(2)}) copy-start(bf16[8,64,64]{2,1,0:T(8,128)(2,1)} %param.13) | copy-start | bytes 196612
  82.0 13.5 %all-to-all-start = ((bf16[32,2,8,192]{3,2,1,0:T(8,128)(2,1)}), bf16[32,2,8,192]{3,2,1,0:T(8,128)(2,1)S(1)}, u32[]{:S(2)}, u32[]{:S(2)}) async-start(bf16[32,2,8,192]{3,2,1,0:T(8,128)(2,1)} %copy.133), calls=%async_computation | async-start | bytes 524288 | tf_op jit(solution)/shard_map/all_to_all | solution.py:10
  85.9 0.5 copy-start.14
  96.2 15.2 %all-to-all-start.3 = ((f32[32,1,640]{2,1,0:T(1,128)}), f32[32,1,640]{2,1,0:T(1,128)S(1)}, u32[]{:S(2)}, u32[]{:S(2)}) async-start(f32[32,1,640]{2,1,0:T(1,128)} %broadcast_in_dim.8), calls=%async_computation.3 | async-start | bytes 163840 | tf_op jit(solution)/shard_map/all_to_all | solution.py:10
  102.6 12.8 %copy-start.12 = (bf16[96,128]{1,0:T(8,128)(2,1)S(1)}, bf16[96,128]{1,0:T(8,128)(2,1)}, u32[]{:S(2)}) copy-start(bf16[96,128]{1,0:T(8,128)(2,1)} %param.15) | copy-start | bytes 73732
  102.7 0.7 copy-start.2
  102.8 0.7 copy-start.4
  111.4 13.6 %all-to-all-start.1 = ((bf16[32,2,8,192]{3,2,1,0:T(8,128)(2,1)}), bf16[32,2,8,192]{3,2,1,0:T(8,128)(2,1)S(1)}, u32[]{:S(2)}, u32[]{:S(2)}) async-start(bf16[32,2,8,192]{3,2,1,0:T(8,128)(2,1)} %pad_maximum_fusion.1), calls=%async_computation.1 | async-start | bytes 524288 | tf_op jit(solution)/shard_map/all_to_all | solution.py:10
  125.6 15.7 %all-to-all-start.5 = ((f32[16,1,256]{2,1,0:T(1,128)}), f32[16,1,256]{2,1,0:T(1,128)}, u32[]{:S(2)}, u32[]{:S(2)}) async-start(f32[16,1,256]{2,1,0:T(1,128)} %broadcast_in_dim.10), calls=%async_computation.5 | async-start | bytes 32768 | tf_op jit(solution)/shard_map/all_to_all | solution.py:14
  134.1 2.3 copy-start.6
  138.4 7.1 %copy-start.3 = (bf16[32,2,8,96]{3,1,0,2:T(2,128)(2,1)S(1)}, bf16[32,2,8,96]{3,1,0,2:T(2,128)(2,1)}, u32[]{:S(2)}) copy-start(bf16[32,2,8,96]{3,1,0,2:T(2,128)(2,1)} %copy-done.2) | copy-start | bytes 294916
  138.4 7.1 %copy-start.5 = (bf16[32,2,8,96]{3,1,0,2:T(2,128)(2,1)S(1)}, bf16[32,2,8,96]{3,1,0,2:T(2,128)(2,1)}, u32[]{:S(2)}) copy-start(bf16[32,2,8,96]{3,1,0,2:T(2,128)(2,1)} %copy-done.4) | copy-start | bytes 294916
  138.4 7.6 %copy-start.7 = (bf16[2,32,8,96]{3,2,0,1:T(8,128)(2,1)S(1)}, bf16[2,32,8,96]{3,2,0,1:T(8,128)(2,1)}, u32[]{:S(2)}) copy-start(bf16[2,32,8,96]{3,2,0,1:T(8,128)(2,1)} %copy-done.6) | copy-start | bytes 294916
  138.4 7.6 %copy-start.11 = (bf16[512,96]{0,1:T(8,128)(2,1)S(1)}, bf16[512,96]{0,1:T(8,128)(2,1)}, u32[]{:S(2)}) copy-start(bf16[512,96]{0,1:T(8,128)(2,1)} %copy-done.10) | copy-start | bytes 294916
  141.3 40.7 %all-to-all-start.4 = ((f32[32,6,1536]{2,1,0:T(8,128)}), f32[32,6,1536]{2,1,0:T(8,128)S(1)}, u32[]{:S(2)}, u32[]{:S(2)}) async-start(f32[32,6,1536]{2,1,0:T(8,128)} %reshape.209), calls=%async_computation.4 | async-start | bytes 3145728 | tf_op jit(solution)/shard_map/all_to_all | solution.py:10
  182.1 27.8 %all-to-all-start.7 = ((f32[16,1,10240]{2,1,0:T(1,128)}), f32[16,1,10240]{2,1,0:T(1,128)S(1)}, u32[]{:S(2)}, u32[]{:S(2)}) async-start(f32[16,1,10240]{2,1,0:T(1,128)} %copy.154), calls=%async_computation.7 | async-start | bytes 1310720 | tf_op jit(solution)/shard_map/all_to_all | solution.py:14
  190.8 26.1 %copy-start.15 = (f32[64]{0:T(128)S(1)}, f32[64]{0:T(128)}, u32[]{:S(2)}) copy-start(f32[64]{0:T(128)} %copy-done.14) | copy-start | bytes 772
  211.5 36.8 %all-to-all-start.6 = ((f32[32,1,9472]{2,1,0:T(1,128)}), f32[32,1,9472]{2,1,0:T(1,128)S(1)}, u32[]{:S(2)}, u32[]{:S(2)}) async-start(f32[32,1,9472]{2,1,0:T(1,128)} %broadcast_in_dim.11), calls=%async_computation.6 | async-start | bytes 2424832 | tf_op jit(solution)/shard_map/all_to_all | solution.py:10
Sparse Core Ops, SparseCore 0:
  10.7 48.6 all-gather.1
where the time goes:
time: 259 us; the launch traced here: 258 us
  waiting for transfers between devices  162 us (63%)
  starting transfers between devices  49 us (19%)
  local copies, waits for them, and re-layouts  15.8 us (6%)
  between operations  14.6 us (6%)
  matrix products  11.5 us (4%)
  other arithmetic  5.15 us (2%)
    all_to_all x6, waiting for transfers between devices, seq_exchange(): return lax.all_to_all(x, 'seq', 0, 0, tiled=True)  92.6 us
    all_gather x1, waiting for transfers between devices, body(): gathered_all = lax.all_gather(packed, 'chan', axis=0, tiled=True)  47.7 us
    all_to_all x6, starting transfers between devices, seq_exchange(): return lax.all_to_all(x, 'seq', 0, 0, tiled=True)  32.8 us
    all_to_all x2, waiting for transfers between devices, chan_exchange(): return lax.all_to_all(x, 'chan', 0, 0, tiled=True)  21.9 us
    all_to_all x2, starting transfers between devices, chan_exchange(): return lax.all_to_all(x, 'chan', 0, 0, tiled=True)  16.2 us
  transfers between devices with their start and end apart: 9, of which 9 were waited for; matrix products, arithmetic and copies ran while one was open for 7% of the time, Pallas kernels for 0%

commit v1 on v0

--- a/solution.py
+++ b/solution.py
@@ -35,7 +35,25 @@
     docs_here = n_doc // n_seq
     me = lax.axis_index("seq")
     packed = jnp.concatenate([tokens, down_latent], axis=1)
-    gathered_all = lax.all_gather(packed, "chan", axis=0, tiled=True)
+    count, index, span = (lax.axis_size("chan"), lax.axis_index("chan"), packed.shape[0])
+    right = [(i, (i + 1) % count) for i in range(count)]
+    downward = [(i, (i - 1) % count) for i in range(count)]
+    gathered_all = jnp.zeros(
+        (*packed.shape[:0], count * span, *packed.shape[0 + 1 :]), packed.dtype
+    )
+    gathered_all = lax.dynamic_update_slice_in_dim(gathered_all, packed, index * span, axis=0)
+    from_left = from_right = packed
+    middle = count // 2
+    for step in range(1, middle + 1):
+        from_left = lax.ppermute(from_left, "chan", right)
+        gathered_all = lax.dynamic_update_slice_in_dim(
+            gathered_all, from_left, (index - step) % count * span, axis=0
+        )
+        if step < count - middle:
+            from_right = lax.ppermute(from_right, "chan", downward)
+            gathered_all = lax.dynamic_update_slice_in_dim(
+                gathered_all, from_right, (index + step) % count * span, axis=0
+            )
     gathered = gathered_all[:, :tok_cols]
     down_full = gathered_all[:, tok_cols:]
     doc_ends = jnp.cumsum(doc_lengths)

time: 259 us -> 246 us (0.950)
  starting transfers between devices: 49 us -> 86.6 us
  waiting for transfers between devices: 162 us -> 125 us
  between operations: 14.6 us -> 1.56 us
    all_gather x1 -> x0, waiting for transfers between devices: 47.7 us -> none  [body(): gathered_all = lax.all_gather(packed, 'chan', axis=0, tiled=True)]
    ppermute x0 -> x15, starting transfers between devices: none -> 32.9 us  [the longest x7 29 us: body(): from_right = lax.ppermute(from_right, 'chan', downward)]
    ppermute x0 -> x15, waiting for transfers between devices: none -> 10.7 us  [the longest x8 9.93 us: body(): from_left = lax.ppermute(from_left, 'chan', right)]
    all_to_all x2, starting transfers between devices: 16.2 us -> 22.3 us  [chan_exchange(): return lax.all_to_all(x, 'chan', 0, 0, tiled=True)]
  transfers between devices with their start and end apart: 9 -> 23, of which waited for: 9 -> 20; matrix products, arithmetic and copies ran while one was open for 7% -> 8% of each run, Pallas kernels for 0% -> 0%
where the time goes in v1:
time: 246 us; the launch traced here: 245 us
  waiting for transfers between devices  125 us (51%)
  starting transfers between devices  86.6 us (35%)
  local copies, waits for them, and re-layouts  17.9 us (7%)
  matrix products  9.78 us (4%)
  other arithmetic  3.53 us (1%)
    all_to_all x6, waiting for transfers between devices, seq_exchange(): return lax.all_to_all(x, 'seq', 0, 0, tiled=True)  92.7 us
    all_to_all x6, starting transfers between devices, seq_exchange(): return lax.all_to_all(x, 'seq', 0, 0, tiled=True)  31.5 us
    ppermute x7, starting transfers between devices, body(): from_right = lax.ppermute(from_right, 'chan', downward)  29 us
    all_to_all x2, starting transfers between devices, chan_exchange(): return lax.all_to_all(x, 'chan', 0, 0, tiled=True)  22.3 us
    all_to_all x2, waiting for transfers between devices, chan_exchange(): return lax.all_to_all(x, 'chan', 0, 0, tiled=True)  22 us
    ppermute x8, waiting for transfers between devices, body(): from_left = lax.ppermute(from_left, 'chan', right)  9.93 us
  transfers between devices with their start and end apart: 23, of which 20 were waited for; matrix products, arithmetic and copies ran while one was open for 8% of the time, Pallas kernels for 0%

profile of v1, /device:TPU:1, one launch (start us, length us, event | category | flops | bytes accessed | tf_op | source)
XLA Modules:
  0.0 244.8 jit_solution(6766438667517531094)
XLA Ops:
  0.6 0.9 constant_dynamic-update-slice_fusion.1
  1.6 0.7 constant_dynamic-update-slice_fusion
  2.3 3.5 %collective-permute-start = (bf16[96,640]{1,0:T(8,128)(2,1)S(1)}, bf16[96,640]{1,0:T(8,128)(2,1)S(1)}, u32[]{:S(2)}, u32[]{:S(2)}) collective-permute-start(bf16[96,640]{1,0:T(8,128)(2,1)S(1)} %constant_dynamic-update-slice_fusion), channel_id=1, source_target_pairs={{0,1},{1,2},{2,3},{3,4},{4,5},{5,6},{6,7},{7,8},{8,9},{9,10},{10,1... | collective-permute-start | bytes 368648 | tf_op jit(solution)/shard_map/ppermute | solution.py:48
  5.8 3.4 %collective-permute-start.1 = (bf16[96,640]{1,0:T(8,128)(2,1)S(1)}, bf16[96,640]{1,0:T(8,128)(2,1)S(1)}, u32[]{:S(2)}, u32[]{:S(2)}) collective-permute-start(bf16[96,640]{1,0:T(8,128)(2,1)S(1)} %constant_dynamic-update-slice_fusion), channel_id=1, source_target_pairs={{0,15},{1,0},{2,1},{3,2},{4,3},{5,4},{6,5},{7,6},{8,7},{9,8},{10,9... | collective-permute-start | bytes 368648 | tf_op jit(solution)/shard_map/ppermute | solution.py:53
  9.2 0.7 copy.140
  10.1 0.7 sub.38
  10.8 1.1 fusion.27
  12.6 3.1 %collective-permute-start.3 = (bf16[96,640]{1,0:T(8,128)(2,1)S(1)}, bf16[96,640]{1,0:T(8,128)(2,1)S(1)}, u32[]{:S(2)}, u32[]{:S(2)}) collective-permute-start(bf16[96,640]{1,0:T(8,128)(2,1)S(1)} %collective-permute-done.1), channel_id=1, source_target_pairs={{0,15},{1,0},{2,1},{3,2},{4,3},{5,4},{6,5},{7,6},{8,7},{9,8},{10,9... | collective-permute-start | bytes 368648 | tf_op jit(solution)/shard_map/ppermute | solution.py:53
  15.8 0.7 collective-permute-done.2
  16.5 0.3 collective-permute-start.4
  16.9 4.3 %collective-permute-start.5 = (bf16[96,640]{1,0:T(8,128)(2,1)S(1)}, bf16[96,640]{1,0:T(8,128)(2,1)S(1)}, u32[]{:S(2)}, u32[]{:S(2)}) collective-permute-start(bf16[96,640]{1,0:T(8,128)(2,1)S(1)} %collective-permute-done.3), channel_id=1, source_target_pairs={{0,15},{1,0},{2,1},{3,2},{4,3},{5,4},{6,5},{7,6},{8,7},{9,8},{10,9... | collective-permute-start | bytes 368648 | tf_op jit(solution)/shard_map/ppermute | solution.py:53
  21.2 0.8 collective-permute-done.4
  22.2 4.5 %collective-permute-start.7 = (bf16[96,640]{1,0:T(8,128)(2,1)S(1)}, bf16[96,640]{1,0:T(8,128)(2,1)S(1)}, u32[]{:S(2)}, u32[]{:S(2)}) collective-permute-start(bf16[96,640]{1,0:T(8,128)(2,1)S(1)} %collective-permute-done.5), channel_id=1, source_target_pairs={{0,15},{1,0},{2,1},{3,2},{4,3},{5,4},{6,5},{7,6},{8,7},{9,8},{10,9... | collective-permute-start | bytes 368648 | tf_op jit(solution)/shard_map/ppermute | solution.py:53
  26.8 0.8 collective-permute-done.6
  27.7 4.5 %collective-permute-start.9 = (bf16[96,640]{1,0:T(8,128)(2,1)S(1)}, bf16[96,640]{1,0:T(8,128)(2,1)S(1)}, u32[]{:S(2)}, u32[]{:S(2)}) collective-permute-start(bf16[96,640]{1,0:T(8,128)(2,1)S(1)} %collective-permute-done.7), channel_id=1, source_target_pairs={{0,15},{1,0},{2,1},{3,2},{4,3},{5,4},{6,5},{7,6},{8,7},{9,8},{10,9... | collective-permute-start | bytes 368648 | tf_op jit(solution)/shard_map/ppermute | solution.py:53
  32.3 0.8 collective-permute-done.8
  33.2 4.5 %collective-permute-start.11 = (bf16[96,640]{1,0:T(8,128)(2,1)S(1)}, bf16[96,640]{1,0:T(8,128)(2,1)S(1)}, u32[]{:S(2)}, u32[]{:S(2)}) collective-permute-start(bf16[96,640]{1,0:T(8,128)(2,1)S(1)} %collective-permute-done.9), channel_id=1, source_target_pairs={{0,15},{1,0},{2,1},{3,2},{4,3},{5,4},{6,5},{7,6},{8,7},{9,8},{10,9... | collective-permute-start | bytes 368648 | tf_op jit(solution)/shard_map/ppermute | solution.py:53
  37.8 0.8 collective-permute-done.10
  38.7 4.5 %collective-permute-start.13 = (bf16[96,640]{1,0:T(8,128)(2,1)S(1)}, bf16[96,640]{1,0:T(8,128)(2,1)S(1)}, u32[]{:S(2)}, u32[]{:S(2)}) collective-permute-start(bf16[96,640]{1,0:T(8,128)(2,1)S(1)} %collective-permute-done.11), channel_id=1, source_target_pairs={{0,15},{1,0},{2,1},{3,2},{4,3},{5,4},{6,5},{7,6},{8,7},{9,8},{10,9... | collective-permute-start | bytes 368648 | tf_op jit(solution)/shard_map/ppermute | solution.py:53
  43.3 0.8 collective-permute-done.12
  44.3 5.3 %collective-permute-done.14 = bf16[96,640]{1,0:T(8,128)(2,1)S(1)} collective-permute-done((bf16[96,640]{1,0:T(8,128)(2,1)S(1)}, bf16[96,640]{1,0:T(8,128)(2,1)S(1)}, u32[]{:S(2)}, u32[]{:S(2)}) %collective-permute-start.14) | collective-permute-done | bytes 122912 | tf_op jit(solution)/shard_map/ppermute | solution.py:48
  49.6 0.4 fusion.4
  50.0 0.4 fusion.17
  50.5 0.3 fusion.16
  50.8 0.4 copy-done.16
  51.3 0.3 fusion.31
  51.7 0.7 all_to_all.39
  52.4 9.7 %all-to-all-start.2 = ((f32[32,1,640]{2,1,0:T(1,128)}), f32[32,1,640]{2,1,0:T(1,128)S(1)}, u32[]{:S(2)}, u32[]{:S(2)}) async-start(f32[32,1,640]{2,1,0:T(1,128)} %all_to_all.39), calls=%async_computation.2 | async-start | bytes 163840 | tf_op jit(solution)/shard_map/all_to_all | solution.py:10
  62.1 1.3 convolution_convert_fusion.2
  64.2 0.7 copy.133
  65.0 6.1 %all-to-all-done.2 = f32[32,1,640]{2,1,0:T(1,128)S(1)} async-done(((f32[32,1,640]{2,1,0:T(1,128)}), f32[32,1,640]{2,1,0:T(1,128)S(1)}, u32[]{:S(2)}, u32[]{:S(2)}) %all-to-all-start.2) | async-done | bytes 81952 | tf_op jit(solution)/shard_map/all_to_all | solution.py:10
  71.0 3.9 %all-to-all-start = ((bf16[32,2,8,192]{3,2,1,0:T(8,128)(2,1)}), bf16[32,2,8,192]{3,2,1,0:T(8,128)(2,1)S(1)}, u32[]{:S(2)}, u32[]{:S(2)}) async-start(bf16[32,2,8,192]{3,2,1,0:T(8,128)(2,1)} %copy.133), calls=%async_computation | async-start | bytes 524288 | tf_op jit(solution)/shard_map/all_to_all | solution.py:10
  75.1 0.3 copy-done.13
  75.5 9.0 %all-to-all-done = bf16[32,2,8,192]{3,2,1,0:T(8,128)(2,1)S(1)} async-done(((bf16[32,2,8,192]{3,2,1,0:T(8,128)(2,1)}), bf16[32,2,8,192]{3,2,1,0:T(8,128)(2,1)S(1)}, u32[]{:S(2)}, u32[]{:S(2)}) %all-to-all-start) | async-done | bytes 196640 | tf_op jit(solution)/shard_map/all_to_all | solution.py:10
  84.6 0.7 broadcast_in_dim.11
  85.2 4.4 %all-to-all-start.3 = ((f32[32,1,640]{2,1,0:T(1,128)}), f32[32,1,640]{2,1,0:T(1,128)S(1)}, u32[]{:S(2)}, u32[]{:S(2)}) async-start(f32[32,1,640]{2,1,0:T(1,128)} %broadcast_in_dim.11), calls=%async_computation.3 | async-start | bytes 163840 | tf_op jit(solution)/shard_map/all_to_all | solution.py:10
  90.0 0.5 copy-done.1
  91.2 0.8 pad_maximum_fusion.1
  92.1 6.5 %all-to-all-done.3 = f32[32,1,640]{2,1,0:T(1,128)S(1)} async-done(((f32[32,1,640]{2,1,0:T(1,128)}), f32[32,1,640]{2,1,0:T(1,128)S(1)}, u32[]{:S(2)}, u32[]{:S(2)}) %all-to-all-start.3) | async-done | bytes 81952 | tf_op jit(solution)/shard_map/all_to_all | solution.py:10
  98.6 3.9 %all-to-all-start.1 = ((bf16[32,2,8,192]{3,2,1,0:T(8,128)(2,1)}), bf16[32,2,8,192]{3,2,1,0:T(8,128)(2,1)S(1)}, u32[]{:S(2)}, u32[]{:S(2)}) async-start(bf16[32,2,8,192]{3,2,1,0:T(8,128)(2,1)} %pad_maximum_fusion.1), calls=%async_computation.1 | async-start | bytes 524288 | tf_op jit(solution)/shard_map/all_to_all | solution.py:10
  103.0 9.1 %all-to-all-done.1 = bf16[32,2,8,192]{3,2,1,0:T(8,128)(2,1)S(1)} async-done(((bf16[32,2,8,192]{3,2,1,0:T(8,128)(2,1)}), bf16[32,2,8,192]{3,2,1,0:T(8,128)(2,1)S(1)}, u32[]{:S(2)}, u32[]{:S(2)}) %all-to-all-start.1) | async-done | bytes 196640 | tf_op jit(solution)/shard_map/all_to_all | solution.py:10
  112.1 0.6 broadcast_in_dim.13
  112.7 14.6 %all-to-all-start.5 = ((f32[16,1,256]{2,1,0:T(1,128)}), f32[16,1,256]{2,1,0:T(1,128)}, u32[]{:S(2)}, u32[]{:S(2)}) async-start(f32[16,1,256]{2,1,0:T(1,128)} %broadcast_in_dim.13), calls=%async_computation.5 | async-start | bytes 32768 | tf_op jit(solution)/shard_map/all_to_all | solution.py:14
  127.8 1.9 fusion.11
  129.7 0.7 fusion.2
  130.4 1.3 reshape.209
  131.8 3.0 %all-to-all-done.5 = f32[16,1,256]{2,1,0:T(1,128)} async-done(((f32[16,1,256]{2,1,0:T(1,128)}), f32[16,1,256]{2,1,0:T(1,128)}, u32[]{:S(2)}, u32[]{:S(2)}) %all-to-all-start.5) | async-done | bytes 16416 | tf_op jit(solution)/shard_map/all_to_all | solution.py:14
  134.7 4.4 %all-to-all-start.4 = ((f32[32,6,1536]{2,1,0:T(8,128)}), f32[32,6,1536]{2,1,0:T(8,128)S(1)}, u32[]{:S(2)}, u32[]{:S(2)}) async-start(f32[32,6,1536]{2,1,0:T(8,128)} %reshape.209), calls=%async_computation.4 | async-start | bytes 3145728 | tf_op jit(solution)/shard_map/all_to_all | solution.py:10
  139.9 0.3 copy.167
  140.3 1.5 copy.154
  141.8 33.9 %all-to-all-done.4 = f32[32,6,1536]{2,1,0:T(8,128)S(1)} async-done(((f32[32,6,1536]{2,1,0:T(8,128)}), f32[32,6,1536]{2,1,0:T(8,128)S(1)}, u32[]{:S(2)}, u32[]{:S(2)}) %all-to-all-start.4) | async-done | bytes 1179680 | tf_op jit(solution)/shard_map/all_to_all | solution.py:10
  175.7 7.7 %all-to-all-start.7 = ((f32[16,1,10240]{2,1,0:T(1,128)}), f32[16,1,10240]{2,1,0:T(1,128)S(1)}, u32[]{:S(2)}, u32[]{:S(2)}) async-start(f32[16,1,10240]{2,1,0:T(1,128)} %copy.154), calls=%async_computation.7 | async-start | bytes 1310720 | tf_op jit(solution)/shard_map/all_to_all | solution.py:14
  183.4 0.8 reduce_sum.38
  184.3 19.0 %all-to-all-done.7 = f32[16,1,10240]{2,1,0:T(1,128)S(1)} async-done(((f32[16,1,10240]{2,1,0:T(1,128)}), f32[16,1,10240]{2,1,0:T(1,128)S(1)}, u32[]{:S(2)}, u32[]{:S(2)}) %all-to-all-start.7) | async-done | bytes 655392 | tf_op jit(solution)/shard_map/all_to_all | solution.py:14
  203.3 1.7 broadcast_in_dim.14
  205.0 5.4 %all-to-all-start.6 = ((f32[32,1,9472]{2,1,0:T(1,128)}), f32[32,1,9472]{2,1,0:T(1,128)S(1)}, u32[]{:S(2)}, u32[]{:S(2)}) async-start(f32[32,1,9472]{2,1,0:T(1,128)} %broadcast_in_dim.14), calls=%async_computation.6 | async-start | bytes 2424832 | tf_op jit(solution)/shard_map/all_to_all | solution.py:10
  210.9 0.9 fusion.39
  211.8 0.4 reduce_sum.39
  212.3 0.6 reshape.216
  212.9 0.7 reshape.217
  213.6 28.2 %all-to-all-done.6 = f32[32,1,9472]{2,1,0:T(1,128)S(1)} async-done(((f32[32,1,9472]{2,1,0:T(1,128)}), f32[32,1,9472]{2,1,0:T(1,128)S(1)}, u32[]{:S(2)}, u32[]{:S(2)}) %all-to-all-start.6) | async-done | bytes 1212448 | tf_op jit(solution)/shard_map/all_to_all | solution.py:10
  242.1 0.9 slice.101
  243.0 0.9 slice.99
  243.9 0.9 fusion.38
  (122 shorter events, 6.7 us)
Async XLA Ops:
  0.6 49.4 %copy-start = (bf16[96,1536]{1,0:T(8,128)(2,1)S(1)}, bf16[96,1536]{1,0:T(8,128)(2,1)}, u32[]{:S(2)}) copy-start(bf16[96,1536]{1,0:T(8,128)(2,1)} %param.10) | copy-start | bytes 884740
  2.3 10.2 %collective-permute-start = (bf16[96,640]{1,0:T(8,128)(2,1)S(1)}, bf16[96,640]{1,0:T(8,128)(2,1)S(1)}, u32[]{:S(2)}, u32[]{:S(2)}) collective-permute-start(bf16[96,640]{1,0:T(8,128)(2,1)S(1)} %constant_dynamic-update-slice_fusion), channel_id=1, source_target_pairs={{0,1},{1,2},{2,3},{3,4},{4,5},{5,6},{6,7},{7,8},{8,9},{9,10},{10,1... | collective-permute-start | bytes 368648 | tf_op jit(solution)/shard_map/ppermute | solution.py:48
  5.8 6.7 %collective-permute-start.1 = (bf16[96,640]{1,0:T(8,128)(2,1)S(1)}, bf16[96,640]{1,0:T(8,128)(2,1)S(1)}, u32[]{:S(2)}, u32[]{:S(2)}) collective-permute-start(bf16[96,640]{1,0:T(8,128)(2,1)S(1)} %constant_dynamic-update-slice_fusion), channel_id=1, source_target_pairs={{0,15},{1,0},{2,1},{3,2},{4,3},{5,4},{6,5},{7,6},{8,7},{9,8},{10,9... | collective-permute-start | bytes 368648 | tf_op jit(solution)/shard_map/ppermute | solution.py:53
  12.5 4.0 %collective-permute-start.2 = (bf16[96,640]{1,0:T(8,128)(2,1)S(1)}, bf16[96,640]{1,0:T(8,128)(2,1)S(1)}, u32[]{:S(2)}, u32[]{:S(2)}) collective-permute-start(bf16[96,640]{1,0:T(8,128)(2,1)S(1)} %collective-permute-done), channel_id=1, source_target_pairs={{0,1},{1,2},{2,3},{3,4},{4,5},{5,6},{6,7},{7,8},{8,9},{9,10},{10,1... | collective-permute-start | bytes 368648 | tf_op jit(solution)/shard_map/ppermute | solution.py:48
  12.6 4.3 %collective-permute-start.3 = (bf16[96,640]{1,0:T(8,128)(2,1)S(1)}, bf16[96,640]{1,0:T(8,128)(2,1)S(1)}, u32[]{:S(2)}, u32[]{:S(2)}) collective-permute-start(bf16[96,640]{1,0:T(8,128)(2,1)S(1)} %collective-permute-done.1), channel_id=1, source_target_pairs={{0,15},{1,0},{2,1},{3,2},{4,3},{5,4},{6,5},{7,6},{8,7},{9,8},{10,9... | collective-permute-start | bytes 368648 | tf_op jit(solution)/shard_map/ppermute | solution.py:53
  16.5 5.5 %collective-permute-start.4 = (bf16[96,640]{1,0:T(8,128)(2,1)S(1)}, bf16[96,640]{1,0:T(8,128)(2,1)S(1)}, u32[]{:S(2)}, u32[]{:S(2)}) collective-permute-start(bf16[96,640]{1,0:T(8,128)(2,1)S(1)} %collective-permute-done.2), channel_id=1, source_target_pairs={{0,1},{1,2},{2,3},{3,4},{4,5},{5,6},{6,7},{7,8},{8,9},{9,10},{10,1... | collective-permute-start | bytes 368648 | tf_op jit(solution)/shard_map/ppermute | solution.py:48
  16.9 5.3 %collective-permute-start.5 = (bf16[96,640]{1,0:T(8,128)(2,1)S(1)}, bf16[96,640]{1,0:T(8,128)(2,1)S(1)}, u32[]{:S(2)}, u32[]{:S(2)}) collective-permute-start(bf16[96,640]{1,0:T(8,128)(2,1)S(1)} %collective-permute-done.3), channel_id=1, source_target_pairs={{0,15},{1,0},{2,1},{3,2},{4,3},{5,4},{6,5},{7,6},{8,7},{9,8},{10,9... | collective-permute-start | bytes 368648 | tf_op jit(solution)/shard_map/ppermute | solution.py:53
  22.0 5.5 %collective-permute-start.6 = (bf16[96,640]{1,0:T(8,128)(2,1)S(1)}, bf16[96,640]{1,0:T(8,128)(2,1)S(1)}, u32[]{:S(2)}, u32[]{:S(2)}) collective-permute-start(bf16[96,640]{1,0:T(8,128)(2,1)S(1)} %collective-permute-done.4), channel_id=1, source_target_pairs={{0,1},{1,2},{2,3},{3,4},{4,5},{5,6},{6,7},{7,8},{8,9},{9,10},{10,1... | collective-permute-start | bytes 368648 | tf_op jit(solution)/shard_map/ppermute | solution.py:48
  22.2 5.5 %collective-permute-start.7 = (bf16[96,640]{1,0:T(8,128)(2,1)S(1)}, bf16[96,640]{1,0:T(8,128)(2,1)S(1)}, u32[]{:S(2)}, u32[]{:S(2)}) collective-permute-start(bf16[96,640]{1,0:T(8,128)(2,1)S(1)} %collective-permute-done.5), channel_id=1, source_target_pairs={{0,15},{1,0},{2,1},{3,2},{4,3},{5,4},{6,5},{7,6},{8,7},{9,8},{10,9... | collective-permute-start | bytes 368648 | tf_op jit(solution)/shard_map/ppermute | solution.py:53
  27.5 5.5 %collective-permute-start.8 = (bf16[96,640]{1,0:T(8,128)(2,1)S(1)}, bf16[96,640]{1,0:T(8,128)(2,1)S(1)}, u32[]{:S(2)}, u32[]{:S(2)}) collective-permute-start(bf16[96,640]{1,0:T(8,128)(2,1)S(1)} %collective-permute-done.6), channel_id=1, source_target_pairs={{0,1},{1,2},{2,3},{3,4},{4,5},{5,6},{6,7},{7,8},{8,9},{9,10},{10,1... | collective-permute-start | bytes 368648 | tf_op jit(solution)/shard_map/ppermute | solution.py:48
  27.7 5.5 %collective-permute-start.9 = (bf16[96,640]{1,0:T(8,128)(2,1)S(1)}, bf16[96,640]{1,0:T(8,128)(2,1)S(1)}, u32[]{:S(2)}, u32[]{:S(2)}) collective-permute-start(bf16[96,640]{1,0:T(8,128)(2,1)S(1)} %collective-permute-done.7), channel_id=1, source_target_pairs={{0,15},{1,0},{2,1},{3,2},{4,3},{5,4},{6,5},{7,6},{8,7},{9,8},{10,9... | collective-permute-start | bytes 368648 | tf_op jit(solution)/shard_map/ppermute | solution.py:53
  32.3 17.8 %copy-start.15 = (bf16[96,512]{1,0:T(8,128)(2,1)S(1)}, bf16[96,512]{1,0:T(8,128)(2,1)}, u32[]{:S(2)}) copy-start(bf16[96,512]{1,0:T(8,128)(2,1)} %param.17) | copy-start | bytes 294916
  33.0 5.5 %collective-permute-start.10 = (bf16[96,640]{1,0:T(8,128)(2,1)S(1)}, bf16[96,640]{1,0:T(8,128)(2,1)S(1)}, u32[]{:S(2)}, u32[]{:S(2)}) collective-permute-start(bf16[96,640]{1,0:T(8,128)(2,1)S(1)} %collective-permute-done.8), channel_id=1, source_target_pairs={{0,1},{1,2},{2,3},{3,4},{4,5},{5,6},{6,7},{7,8},{8,9},{9,10},{10,1... | collective-permute-start | bytes 368648 | tf_op jit(solution)/shard_map/ppermute | solution.py:48
  33.2 5.5 %collective-permute-start.11 = (bf16[96,640]{1,0:T(8,128)(2,1)S(1)}, bf16[96,640]{1,0:T(8,128)(2,1)S(1)}, u32[]{:S(2)}, u32[]{:S(2)}) collective-permute-start(bf16[96,640]{1,0:T(8,128)(2,1)S(1)} %collective-permute-done.9), channel_id=1, source_target_pairs={{0,15},{1,0},{2,1},{3,2},{4,3},{5,4},{6,5},{7,6},{8,7},{9,8},{10,9... | collective-permute-start | bytes 368648 | tf_op jit(solution)/shard_map/ppermute | solution.py:53
  38.6 5.5 %collective-permute-start.12 = (bf16[96,640]{1,0:T(8,128)(2,1)S(1)}, bf16[96,640]{1,0:T(8,128)(2,1)S(1)}, u32[]{:S(2)}, u32[]{:S(2)}) collective-permute-start(bf16[96,640]{1,0:T(8,128)(2,1)S(1)} %collective-permute-done.10), channel_id=1, source_target_pairs={{0,1},{1,2},{2,3},{3,4},{4,5},{5,6},{6,7},{7,8},{8,9},{9,10},{10,1... | collective-permute-start | bytes 368648 | tf_op jit(solution)/shard_map/ppermute | solution.py:48
  38.7 5.5 %collective-permute-start.13 = (bf16[96,640]{1,0:T(8,128)(2,1)S(1)}, bf16[96,640]{1,0:T(8,128)(2,1)S(1)}, u32[]{:S(2)}, u32[]{:S(2)}) collective-permute-start(bf16[96,640]{1,0:T(8,128)(2,1)S(1)} %collective-permute-done.11), channel_id=1, source_target_pairs={{0,15},{1,0},{2,1},{3,2},{4,3},{5,4},{6,5},{7,6},{8,7},{9,8},{10,9... | collective-permute-start | bytes 368648 | tf_op jit(solution)/shard_map/ppermute | solution.py:53
  44.1 5.5 %collective-permute-start.14 = (bf16[96,640]{1,0:T(8,128)(2,1)S(1)}, bf16[96,640]{1,0:T(8,128)(2,1)S(1)}, u32[]{:S(2)}, u32[]{:S(2)}) collective-permute-start(bf16[96,640]{1,0:T(8,128)(2,1)S(1)} %collective-permute-done.12), channel_id=1, source_target_pairs={{0,1},{1,2},{2,3},{3,4},{4,5},{5,6},{6,7},{7,8},{8,9},{9,10},{10,1... | collective-permute-start | bytes 368648 | tf_op jit(solution)/shard_map/ppermute | solution.py:48
  50.5 0.7 copy-start.16
  50.5 13.0 %copy-start.7 = (bf16[2,256,256]{2,1,0:T(8,128)(2,1)S(1)}, bf16[2,256,256]{2,1,0:T(8,128)(2,1)}, u32[]{:S(2)}) copy-start(bf16[2,256,256]{2,1,0:T(8,128)(2,1)} %param.12) | copy-start | bytes 786436
  52.4 18.6 %all-to-all-start.2 = ((f32[32,1,640]{2,1,0:T(1,128)}), f32[32,1,640]{2,1,0:T(1,128)S(1)}, u32[]{:S(2)}, u32[]{:S(2)}) async-start(f32[32,1,640]{2,1,0:T(1,128)} %all_to_all.39), calls=%async_computation.2 | async-start | bytes 163840 | tf_op jit(solution)/shard_map/all_to_all | solution.py:10
  62.1 12.8 %copy-start.12 = (s32[64]{0:T(128)S(1)}, s32[64]{0:T(128)}, u32[]{:S(2)}) copy-start(s32[64]{0:T(128)} %param.16) | copy-start | bytes 772
  63.5 0.6 copy-start.9
  63.5 27.0 %copy-start.8 = (bf16[8,64,64]{2,1,0:T(8,128)(2,1)S(1)}, bf16[8,64,64]{2,1,0:T(8,128)(2,1)}, u32[]{:S(2)}) copy-start(bf16[8,64,64]{2,1,0:T(8,128)(2,1)} %param.13) | copy-start | bytes 196612
  71.0 13.5 %all-to-all-start = ((bf16[32,2,8,192]{3,2,1,0:T(8,128)(2,1)}), bf16[32,2,8,192]{3,2,1,0:T(8,128)(2,1)S(1)}, u32[]{:S(2)}, u32[]{:S(2)}) async-start(bf16[32,2,8,192]{3,2,1,0:T(8,128)(2,1)} %copy.133), calls=%async_computation | async-start | bytes 524288 | tf_op jit(solution)/shard_map/all_to_all | solution.py:10
  74.9 27.7 %copy-start.11 = (bf16[96,128]{1,0:T(8,128)(2,1)S(1)}, bf16[96,128]{1,0:T(8,128)(2,1)}, u32[]{:S(2)}) copy-start(bf16[96,128]{1,0:T(8,128)(2,1)} %param.15) | copy-start | bytes 73732
  74.9 0.5 copy-start.13
  85.2 13.3 %all-to-all-start.3 = ((f32[32,1,640]{2,1,0:T(1,128)}), f32[32,1,640]{2,1,0:T(1,128)S(1)}, u32[]{:S(2)}, u32[]{:S(2)}) async-start(f32[32,1,640]{2,1,0:T(1,128)} %broadcast_in_dim.11), calls=%async_computation.3 | async-start | bytes 163840 | tf_op jit(solution)/shard_map/all_to_all | solution.py:10
  89.8 0.6 copy-start.1
  90.0 0.7 copy-start.3
  98.6 13.5 %all-to-all-start.1 = ((bf16[32,2,8,192]{3,2,1,0:T(8,128)(2,1)}), bf16[32,2,8,192]{3,2,1,0:T(8,128)(2,1)S(1)}, u32[]{:S(2)}, u32[]{:S(2)}) async-start(bf16[32,2,8,192]{3,2,1,0:T(8,128)(2,1)} %pad_maximum_fusion.1), calls=%async_computation.1 | async-start | bytes 524288 | tf_op jit(solution)/shard_map/all_to_all | solution.py:10
  112.7 22.0 %all-to-all-start.5 = ((f32[16,1,256]{2,1,0:T(1,128)}), f32[16,1,256]{2,1,0:T(1,128)}, u32[]{:S(2)}, u32[]{:S(2)}) async-start(f32[16,1,256]{2,1,0:T(1,128)} %broadcast_in_dim.13), calls=%async_computation.5 | async-start | bytes 32768 | tf_op jit(solution)/shard_map/all_to_all | solution.py:14
  127.4 2.3 copy-start.5
  131.7 7.4 %copy-start.2 = (bf16[32,2,8,96]{3,1,0,2:T(2,128)(2,1)S(1)}, bf16[32,2,8,96]{3,1,0,2:T(2,128)(2,1)}, u32[]{:S(2)}) copy-start(bf16[32,2,8,96]{3,1,0,2:T(2,128)(2,1)} %copy-done.1) | copy-start | bytes 294916
  131.7 7.4 %copy-start.4 = (bf16[32,2,8,96]{3,1,0,2:T(2,128)(2,1)S(1)}, bf16[32,2,8,96]{3,1,0,2:T(2,128)(2,1)}, u32[]{:S(2)}) copy-start(bf16[32,2,8,96]{3,1,0,2:T(2,128)(2,1)} %copy-done.3) | copy-start | bytes 294916
  131.7 7.9 %copy-start.6 = (bf16[2,32,8,96]{3,2,0,1:T(8,128)(2,1)S(1)}, bf16[2,32,8,96]{3,2,0,1:T(8,128)(2,1)}, u32[]{:S(2)}) copy-start(bf16[2,32,8,96]{3,2,0,1:T(8,128)(2,1)} %copy-done.5) | copy-start | bytes 294916
  131.8 7.9 %copy-start.10 = (bf16[512,96]{0,1:T(8,128)(2,1)S(1)}, bf16[512,96]{0,1:T(8,128)(2,1)}, u32[]{:S(2)}) copy-start(bf16[512,96]{0,1:T(8,128)(2,1)} %copy-done.9) | copy-start | bytes 294916
  134.7 41.0 %all-to-all-start.4 = ((f32[32,6,1536]{2,1,0:T(8,128)}), f32[32,6,1536]{2,1,0:T(8,128)S(1)}, u32[]{:S(2)}, u32[]{:S(2)}) async-start(f32[32,6,1536]{2,1,0:T(8,128)} %reshape.209), calls=%async_computation.4 | async-start | bytes 3145728 | tf_op jit(solution)/shard_map/all_to_all | solution.py:10
  175.7 27.6 %all-to-all-start.7 = ((f32[16,1,10240]{2,1,0:T(1,128)}), f32[16,1,10240]{2,1,0:T(1,128)S(1)}, u32[]{:S(2)}, u32[]{:S(2)}) async-start(f32[16,1,10240]{2,1,0:T(1,128)} %copy.154), calls=%async_computation.7 | async-start | bytes 1310720 | tf_op jit(solution)/shard_map/all_to_all | solution.py:14
  184.3 26.1 %copy-start.14 = (f32[64]{0:T(128)S(1)}, f32[64]{0:T(128)}, u32[]{:S(2)}) copy-start(f32[64]{0:T(128)} %copy-done.13) | copy-start | bytes 772
  205.0 36.8 %all-to-all-start.6 = ((f32[32,1,9472]{2,1,0:T(1,128)}), f32[32,1,9472]{2,1,0:T(1,128)S(1)}, u32[]{:S(2)}, u32[]{:S(2)}) async-start(f32[32,1,9472]{2,1,0:T(1,128)} %broadcast_in_dim.14), calls=%async_computation.6 | async-start | bytes 2424832 | tf_op jit(solution)/shard_map/all_to_all | solution.py:10
